TPU v7x, 256 devices: a whole 4x4x8 slice. The times are simulated.
256 devices in a mesh: lat: 16 (over x_lo, z), lon: 16 (over y, x_hi, core).
Axes of the slice: x: 4 (x_hi: 2, x_lo: 2; x = x_hi * 2 + x_lo), y: 4, z: 8, core: 2. Of those that a mesh axis runs over, the one named last changes fastest.
Arguments:
- field_in: bfloat16 [160, 1536, 512], P('lat', 'lon'), may hold values from -6 to 6
- kernel_taps: bfloat16 [3, 160, 3, 33], P(None, 'lat'), may hold values from -0.8984375 to 0.8984375
- row_reach: int32 [160], P('lat'), may hold values from 1 to 16, as said below
- mix_weight: bfloat16 [3, 512, 512], replicated, may hold values from -0.15625 to 0.15625
- up_weight: bfloat16 [512, 1024], replicated, may hold values from -0.25 to 0.25
- down_weight: bfloat16 [1024, 512], replicated, may hold values from -0.1875 to 0.1875
- cotangent: bfloat16 [160, 1536, 512], P('lat', 'lon'), may hold values from -6 to 6
Outputs:
- block_out: bfloat16 [160, 1536, 512], P('lat', 'lon')
- grad_field: bfloat16 [160, 1536, 512], P('lat', 'lon')
- grad_mix: bfloat16 [3, 512, 512], replicated
- grad_up: bfloat16 [512, 1024], replicated
- grad_down: bfloat16 [1024, 512], replicated
Inputs may be any that keep to these rules, and one draw needn't show every extreme that they name: `row_reach`: how many longitude cells each latitude row's kernel reaches on either side.
All inputs are finite; a program needn't handle non-finite values.
Results may differ from a plain program's by a relative error of at most 0.0068.
Values may be sent and summed in bfloat16 or wider, within the bound.
A program may use at most 128 MiB of HBM per device.

v0:
```python
import math
import jax
import jax.numpy as jnp
from jax import lax
from jax.sharding import PartitionSpec as P

inv_root_two = 0.7071067811865476
inv_root_tau = 0.3989422804014327


def extended_2(x, sides, width, wrap):
    for axis, dim in sides:
        devices, length = (lax.axis_size(axis), x.shape[dim])
        up = [(i, (i + 1) % devices) for i in range(devices if wrap else devices - 1)]
        down = [(j, i) for i, j in up]
        last = lax.slice_in_dim(x, length - width, length, axis=dim)
        leading = lax.slice_in_dim(x, 0, width, axis=dim)
        before = lax.ppermute(last, axis, up)
        after = lax.ppermute(leading, axis, down)
        x = jnp.concatenate([before, x, after], axis=dim)
    return x


def shifted(block, axis, distance):
    devices = range(lax.axis_size(axis))
    route = [((i - distance) % len(devices), i) for i in devices]
    return lax.ppermute(block, axis, route)


def gelu_exact(value):
    return 0.5 * value * (1.0 + jax.scipy.special.erf(value * inv_root_two))


def gelu_slope(value):
    return (
        0.5 * (1.0 + jax.scipy.special.erf(value * inv_root_two))
        + value * jnp.exp(-0.5 * value * value) * inv_root_tau
    )


def local(field_in, kernel_taps, row_reach, mix_weight, up_weight, down_weight, cotangent):
    lat_rows, lon_cols, channels = field_in.shape
    basis_count = kernel_taps.shape[0]
    tap_count = kernel_taps.shape[3]
    reach_cells = (tap_count - 1) // 2
    lat_count = lax.axis_size("lat")
    lon_count = lax.axis_size("lon")
    lat_place = lax.axis_index("lat")
    north_pole = lat_place == 0
    south_pole = lat_place == lat_count - 1
    first_pass = extended_2(field_in, (("lat", 0),), 1, False)
    extended = extended_2(first_pass, (("lon", 1),), reach_cells, True)
    across = shifted(jnp.stack([extended[1], extended[lat_rows]]), "lon", lon_count // 2)
    extended = extended.at[0].set(jnp.where(north_pole, across[0], extended[0]))
    extended = extended.at[lat_rows + 1].set(
        jnp.where(south_pole, across[1], extended[lat_rows + 1])
    )
    padded_width = lon_cols + 2 * reach_cells
    offsets = jnp.arange(tap_count, dtype=jnp.int32) - reach_cells
    tap_mask = jnp.abs(offsets)[None, :] <= row_reach[:, None]
    masked_taps = jnp.where(
        tap_mask[None, :, None, :], kernel_taps, jnp.zeros((), kernel_taps.dtype)
    )
    selector = (
        jnp.arange(padded_width, dtype=jnp.int32)[None, :, None]
        - jnp.arange(lon_cols, dtype=jnp.int32)[:, None, None]
        == jnp.arange(tap_count, dtype=jnp.int32)[None, None, :]
    ).astype(jnp.bfloat16)
    band_matrix = jnp.einsum(
        "krdt,jat->krjda", masked_taps, selector, preferred_element_type=jnp.float32
    ).astype(jnp.bfloat16)
    windows = jnp.stack(
        [extended[0:lat_rows], extended[1 : lat_rows + 1], extended[2 : lat_rows + 2]], axis=1
    )
    features = jnp.einsum(
        "krjda,rdac->krjc", band_matrix, windows, preferred_element_type=jnp.float32
    ).astype(jnp.bfloat16)
    points = lat_rows * lon_cols
    flat_features = features.reshape(basis_count, points, channels)
    flat_field = field_in.reshape(points, channels)
    conv_sum = jnp.einsum(
        "kpc,kcd->pd", flat_features, mix_weight, preferred_element_type=jnp.float32
    )
    hidden = (flat_field.astype(jnp.float32) + conv_sum).astype(jnp.bfloat16)
    pre_act = jnp.dot(hidden, up_weight, preferred_element_type=jnp.float32)
    activated = gelu_exact(pre_act).astype(jnp.bfloat16)
    block_out = (
        hidden.astype(jnp.float32)
        + jnp.dot(activated, down_weight, preferred_element_type=jnp.float32)
    ).astype(jnp.bfloat16)
    grad_rows = cotangent.reshape(points, channels)
    act_grad = lax.dot_general(
        grad_rows, down_weight, (((1,), (1,)), ((), ())), preferred_element_type=jnp.float32
    )
    pre_grad = (act_grad * gelu_slope(pre_act)).astype(jnp.bfloat16)
    down_local = lax.dot_general(
        activated, grad_rows, (((0,), (0,)), ((), ())), preferred_element_type=jnp.float32
    )
    up_local = lax.dot_general(
        hidden, pre_grad, (((0,), (0,)), ((), ())), preferred_element_type=jnp.float32
    )
    hidden_grad = (
        grad_rows.astype(jnp.float32)
        + lax.dot_general(
            pre_grad, up_weight, (((1,), (1,)), ((), ())), preferred_element_type=jnp.float32
        )
    ).astype(jnp.bfloat16)
    mix_local = jnp.einsum(
        "kpc,pd->kcd", flat_features, hidden_grad, preferred_element_type=jnp.float32
    )
    feat_grad = jnp.einsum(
        "pd,kcd->kpc", hidden_grad, mix_weight, preferred_element_type=jnp.float32
    ).astype(jnp.bfloat16)
    feat_grad_rows = feat_grad.reshape(basis_count, lat_rows, lon_cols, channels)
    spread = jnp.einsum(
        "krjda,krjc->rdac", band_matrix, feat_grad_rows, preferred_element_type=jnp.float32
    )
    pulled = (
        jnp.pad(spread[:, 0], ((0, 2), (0, 0), (0, 0)))
        + jnp.pad(spread[:, 1], ((1, 1), (0, 0), (0, 0)))
        + jnp.pad(spread[:, 2], ((2, 0), (0, 0), (0, 0)))
    )
    returned = shifted(
        jnp.stack([pulled[0], pulled[lat_rows + 1]]).astype(jnp.bfloat16), "lon", lon_count // 2
    ).astype(jnp.float32)
    pulled = pulled.at[1].add(jnp.where(north_pole, returned[0], jnp.zeros_like(returned[0])))
    pulled = pulled.at[lat_rows].add(
        jnp.where(south_pole, returned[1], jnp.zeros_like(returned[1]))
    )
    col_rims = jnp.concatenate(
        [pulled[:, :reach_cells], pulled[:, lon_cols + reach_cells :]], axis=1
    )
    col_edges = extended_2(col_rims.astype(jnp.bfloat16), (("lon", 1),), reach_cells, True).astype(
        col_rims.dtype
    )
    interior = pulled[:, reach_cells : reach_cells + lon_cols]
    interior = interior.at[:, :reach_cells].add(col_edges[:, :reach_cells])
    interior = interior.at[:, lon_cols - reach_cells :].add(col_edges[:, 3 * reach_cells :])
    row_edges = extended_2(
        jnp.stack([interior[0], interior[lat_rows + 1]]).astype(jnp.bfloat16),
        (("lat", 0),),
        1,
        False,
    ).astype(jnp.float32)
    adjoint = interior[1 : lat_rows + 1]
    adjoint = adjoint.at[0].add(row_edges[0])
    adjoint = adjoint.at[lat_rows - 1].add(row_edges[3])
    grad_field = (
        hidden_grad.astype(jnp.float32).reshape(lat_rows, lon_cols, channels) + adjoint
    ).astype(jnp.bfloat16)
    grad_scale = 1.0 / math.sqrt(points * lat_count * lon_count)
    mix_total, up_total, down_total = lax.psum((mix_local, up_local, down_local), ("lat", "lon"))
    mix_out = (mix_total * grad_scale).astype(jnp.bfloat16)
    up_out = (up_total * grad_scale).astype(jnp.bfloat16)
    down_out = (down_total * grad_scale).astype(jnp.bfloat16)
    return (block_out.reshape(lat_rows, lon_cols, channels), grad_field, mix_out, up_out, down_out)


def solution(mesh):
    placed = (
        P("lat", "lon", None),
        P(None, "lat", None, None),
        P("lat"),
        P(),
        P(),
        P(),
        P("lat", "lon", None),
    )
    return jax.shard_map(
        local,
        mesh=mesh,
        in_specs=placed,
        out_specs=(P("lat", "lon", None), P("lat", "lon", None), P(), P(), P()),
        check_vma=False,
    )
```

profile of v0, /device:TPU:8, one launch (start us, length us, event | category | flops | bytes accessed | tf_op | source)
XLA Modules:
  0.0 365.4 jit_solution(5280903188768959156)
XLA Ops:
  7.2 0.0 copy-start
  7.2 0.0 all-reduce.6.cloned.1.call-start
  7.2 1.1 fusion.45
  8.3 1.3 collective-permute-start.1
  9.6 4.6 %collective-permute-start = (bf16[1,96,512]{2,1,0:T(8,128)(2,1)S(1)}, bf16[1,96,512]{2,1,0:T(8,128)(2,1)S(1)}, u32[]{:S(2)}, u32[]{:S(2)}) collective-permute-start(bf16[1,96,512]{2,1,0:T(8,128)(2,1)S(1)} %get-tuple-element.123), channel_id=1, source_target_pairs={{0,16},{16,32},{32,48},{48,64},{64,80},{80,96},{96,112},{112,128},... | collective-permute-start | bytes 294920 | tf_op jit(solution)/shard_map/ppermute | solution.py:18
  14.2 0.7 broadcast_compare_fusion
  14.9 1.4 collective-permute-done
  16.4 1.3 constant_dynamic-update-slice_fusion.1
  17.7 0.0 collective-permute-done.1
  17.7 0.1 collective-permute-start.2
  17.8 4.1 %collective-permute-start.3 = (bf16[12,16,512]{2,1,0:T(8,128)(2,1)S(1)}, bf16[12,16,512]{2,1,0:T(8,128)(2,1)S(1)}, u32[]{:S(2)}, u32[]{:S(2)}) collective-permute-start(bf16[12,16,512]{2,1,0:T(8,128)(2,1)S(1)} %get-tuple-element.121), channel_id=1, source_target_pairs={{1,0},{2,1},{3,2},{4,3},{5,4},{6,5},{7,6},{8,7},{9,8},{10,9},{11,1... | collective-permute-start | bytes 589832 | tf_op jit(solution)/shard_map/ppermute | solution.py:19
  22.0 6.0 %collective-permute-done.2 = bf16[12,16,512]{2,1,0:T(8,128)(2,1)S(1)} collective-permute-done((bf16[12,16,512]{2,1,0:T(8,128)(2,1)S(1)}, bf16[12,16,512]{2,1,0:T(8,128)(2,1)S(1)}, u32[]{:S(2)}, u32[]{:S(2)}) %collective-permute-start.2) | collective-permute-done | bytes 196640 | tf_op jit(solution)/shard_map/ppermute | solution.py:18
  28.0 0.0 collective-permute-done.3
  28.0 0.2 pad_maximum_fusion
  28.2 2.1 collective-permute-start.4
  30.3 1.1 convert_bitcast_fusion
  31.4 7.1 %collective-permute-done.4 = bf16[2,128,512]{2,1,0:T(8,128)(2,1)S(1)} collective-permute-done((bf16[2,128,512]{2,1,0:T(8,128)(2,1)S(1)}, bf16[2,128,512]{2,1,0:T(8,128)(2,1)S(1)}, u32[]{:S(2)}, u32[]{:S(2)}) %collective-permute-start.4) | collective-permute-done | bytes 262176 | tf_op jit(solution)/shard_map/ppermute | solution.py:27
  38.6 0.4 slice_bitcast_fusion.5
  39.1 1.9 fusion.11
  41.0 0.0 copy-start.6
  41.0 0.2 copy.25
  41.2 1.0 copy-done.6
  42.2 1.7 fusion.19
  44.0 0.0 copy-start.7
  44.0 0.0 copy-start.13
  44.0 0.0 copy-start.15
  44.0 4.1 %multiply_convert_fusion = (bf16[960,1024]{1,0:T(8,128)(2,1)S(1)}, f32[960,1024]{1,0:T(8,128)S(1)}) fusion(bf16[960,512]{1,0:T(8,128)(2,1)S(1)} %fusion.19, bf16[512,1024]{1,0:T(8,128)(2,1)S(1)} %copy-done.12), kind=kOutput, calls=%fused_computation.14 | convolution fusion | flops 1011548160 | bytes 7929856 | tf_op jit(solution)/shard_map/dot_general | solution.py:85
  48.2 2.5 fusion.5
  50.6 1.3 add_convert_fusion
  51.9 0.0 copy-start.9
  51.9 2.6 fusion.46
  54.5 3.5 fusion.22
  58.0 3.3 convolution_convert_fusion
  61.4 2.7 fusion.47
  64.0 4.1 %convolution_bitcast_fusion = f32[10,3,128,512]{3,2,0,1:T(8,128)S(1)} fusion(bf16[3,10,96,512]{3,2,1,0:T(8,128)(2,1)} %bitcast.83, bf16[3,10,96,3,128]{4,1,3,0,2:T(8,128)(2,1)S(1)} %copy-done.3), kind=kOutput, calls=%fused_computation.19 | convolution fusion | flops 1132462080 | bytes 13025280 | tf_op jit(solution)/shard_map/krjda,krjc->rdac/dot_general | solution.py:115
  68.1 3.7 %slice_bitcast_fusion.2 = (f32[10,128,512]{2,1,0:T(8,128)S(1)}, f32[10,128,512]{2,1,0:T(8,128)}, f32[10,128,512]{2,1,0:T(8,128)}) fusion(f32[10,3,128,512]{3,2,0,1:T(8,128)S(1)} %convolution_bitcast_fusion), kind=kLoop, calls=%fused_computation.25 | loop fusion | bytes 15728640 | tf_op jit(solution)/shard_map/squeeze | solution.py:119
  71.8 0.0 all-reduce.6.cloned.1.call-update
  71.9 3.7 %fusion.39 = (bf16[12,128,512]{2,1,0:T(8,128)(2,1)S(1)}, f32[12,128,512]{2,1,0:T(8,128)S(1)}) fusion(f32[10,128,512]{2,1,0:T(8,128)} %get-tuple-element.108, f32[10,128,512]{2,1,0:T(8,128)} %get-tuple-element.107, f32[10,128,512]{2,1,0:T(8,128)S(1)} %get-tuple-element.106), kind=kLoop, calls=%fused_computation.83 | loop fusion | flops 2359296 | bytes 12582912 | tf_op jit(solution)/shard_map/convert.13
  75.6 1.3 collective-permute-start.5
  76.9 8.7 %collective-permute-done.5 = bf16[2,128,512]{2,1,0:T(8,128)(2,1)S(1)} collective-permute-done((bf16[2,128,512]{2,1,0:T(8,128)(2,1)S(1)}, bf16[2,128,512]{2,1,0:T(8,128)(2,1)S(1)}, u32[]{:S(2)}, u32[]{:S(2)}) %collective-permute-start.5) | collective-permute-done | bytes 262176 | tf_op jit(solution)/shard_map/ppermute | solution.py:27
  85.7 0.1 fusion.31
  85.8 0.1 fusion.29
  85.9 0.2 convert.21
  86.2 0.1 collective-permute-start.6
  86.2 4.1 %collective-permute-start.7 = (bf16[12,16,512]{2,1,0:T(8,128)(2,1)S(1)}, bf16[12,16,512]{2,1,0:T(8,128)(2,1)S(1)}, u32[]{:S(2)}, u32[]{:S(2)}) collective-permute-start(bf16[12,16,512]{2,1,0:T(8,128)(2,1)S(1)} %get-tuple-element.110), channel_id=1, source_target_pairs={{1,0},{2,1},{3,2},{4,3},{5,4},{6,5},{7,6},{8,7},{9,8},{10,9},{11,1... | collective-permute-start | bytes 589832 | tf_op jit(solution)/shard_map/ppermute | solution.py:19
  90.4 0.2 slice.334
  90.6 4.2 %collective-permute-done.6 = bf16[12,16,512]{2,1,0:T(8,128)(2,1)S(1)} collective-permute-done((bf16[12,16,512]{2,1,0:T(8,128)(2,1)S(1)}, bf16[12,16,512]{2,1,0:T(8,128)(2,1)S(1)}, u32[]{:S(2)}, u32[]{:S(2)}) %collective-permute-start.6) | collective-permute-done | bytes 196640 | tf_op jit(solution)/shard_map/ppermute | solution.py:18
  94.8 0.0 collective-permute-done.7
  94.8 0.1 fusion.27
  94.9 0.1 fusion.26
  95.0 0.0 copy-start.8
  95.0 0.0 copy-start.14
  95.0 0.2 convert.22
  95.2 4.0 %collective-permute-start.8 = (bf16[1,96,512]{2,1,0:T(8,128)(2,1)S(1)}, bf16[1,96,512]{2,1,0:T(8,128)(2,1)S(1)}, u32[]{:S(2)}, u32[]{:S(2)}) collective-permute-start(bf16[1,96,512]{2,1,0:T(8,128)(2,1)S(1)} %get-tuple-element.118), channel_id=1, source_target_pairs={{0,16},{16,32},{32,48},{48,64},{64,80},{80,96},{96,112},{112,128},... | collective-permute-start | bytes 294920 | tf_op jit(solution)/shard_map/ppermute | solution.py:18
  99.2 1.3 collective-permute-start.9
  100.5 2.1 add_convert_fusion.1
  102.6 0.2 slice.339
  102.8 4.0 %collective-permute-done.9 = bf16[1,96,512]{2,1,0:T(8,128)(2,1)S(1)} collective-permute-done((bf16[1,96,512]{2,1,0:T(8,128)(2,1)S(1)}, bf16[1,96,512]{2,1,0:T(8,128)(2,1)S(1)}, u32[]{:S(2)}, u32[]{:S(2)}) %collective-permute-start.9) | collective-permute-done | bytes 98336 | tf_op jit(solution)/shard_map/ppermute | solution.py:19
  106.9 1.3 fusion.18
  108.2 243.5 %all-reduce.6.cloned.1.call-done = (f32[3,512,512]{2,1,0:T(8,128)}, f32[512,1024]{1,0:T(8,128)}, f32[1024,512]{1,0:T(8,128)}) async-done(((f32[3,512,512]{2,1,0:T(8,128)}, f32[512,1024]{1,0:T(8,128)}, f32[1024,512]{1,0:T(8,128)}), (f32[3,512,512]{2,1,0:T(8,128)}, f32[512,1024]{1,0:T(8,128)}, f32[1024,512]{1,0:T(8,128)})) %all-reduce.6.cloned.1.call-update) | async-done | bytes 7340048 | tf_op jit(solution)/shard_map/psum | solution.py:152
  351.7 3.6 multiply_convert_fusion.1
  355.3 1.2 multiply_convert_fusion.3
  356.5 0.7 copy-done.4
  357.3 1.3 multiply_convert_fusion.2
  (44 shorter events, 0.5 us)
Async XLA Ops:
  7.2 34.1 %copy-start = (bf16[3,512,512]{2,1,0:T(8,128)(2,1)S(1)}, bf16[3,512,512]{2,1,0:T(8,128)(2,1)}, u32[]{:S(2)}) copy-start(bf16[3,512,512]{2,1,0:T(8,128)(2,1)} %param.26) | copy-start | bytes 4718596
  7.2 14.8 %copy-start.11 = (bf16[3,10,3,33]{3,2,1,0:T(4,128)(2,1)S(1)}, bf16[3,10,3,33]{3,2,1,0:T(4,128)(2,1)}, u32[]{:S(2)}) copy-start(bf16[3,10,3,33]{3,2,1,0:T(4,128)(2,1)} %param.24) | copy-start | bytes 17824
  7.2 344.5 %all-reduce.6.cloned.1.call-start = ((), (), s32[]{:S(2)}) async-start(), calls=%async_computation | async-start | bytes 14680064 | tf_op jit(solution)/shard_map/psum | solution.py:152
  8.3 9.4 %collective-permute-start.1 = (bf16[1,96,512]{2,1,0:T(8,128)(2,1)S(1)}, bf16[1,96,512]{2,1,0:T(8,128)(2,1)S(1)}, u32[]{:S(2)}, u32[]{:S(2)}) collective-permute-start(bf16[1,96,512]{2,1,0:T(8,128)(2,1)S(1)} %get-tuple-element.122), channel_id=1, source_target_pairs={{16,0},{32,16},{48,32},{64,48},{80,64},{96,80},{112,96},{128,112},... | collective-permute-start | bytes 294920 | tf_op jit(solution)/shard_map/ppermute | solution.py:19
  9.6 6.8 %collective-permute-start = (bf16[1,96,512]{2,1,0:T(8,128)(2,1)S(1)}, bf16[1,96,512]{2,1,0:T(8,128)(2,1)S(1)}, u32[]{:S(2)}, u32[]{:S(2)}) collective-permute-start(bf16[1,96,512]{2,1,0:T(8,128)(2,1)S(1)} %get-tuple-element.123), channel_id=1, source_target_pairs={{0,16},{16,32},{32,48},{48,64},{64,80},{80,96},{96,112},{112,128},... | collective-permute-start | bytes 294920 | tf_op jit(solution)/shard_map/ppermute | solution.py:18
  17.7 10.2 %collective-permute-start.2 = (bf16[12,16,512]{2,1,0:T(8,128)(2,1)S(1)}, bf16[12,16,512]{2,1,0:T(8,128)(2,1)S(1)}, u32[]{:S(2)}, u32[]{:S(2)}) collective-permute-start(bf16[12,16,512]{2,1,0:T(8,128)(2,1)S(1)} %get-tuple-element.120), channel_id=1, source_target_pairs={{0,1},{1,2},{2,3},{3,4},{4,5},{5,6},{6,7},{7,8},{8,9},{9,10},{10,1... | collective-permute-start | bytes 589832 | tf_op jit(solution)/shard_map/ppermute | solution.py:18
  17.8 10.2 %collective-permute-start.3 = (bf16[12,16,512]{2,1,0:T(8,128)(2,1)S(1)}, bf16[12,16,512]{2,1,0:T(8,128)(2,1)S(1)}, u32[]{:S(2)}, u32[]{:S(2)}) collective-permute-start(bf16[12,16,512]{2,1,0:T(8,128)(2,1)S(1)} %get-tuple-element.121), channel_id=1, source_target_pairs={{1,0},{2,1},{3,2},{4,3},{5,4},{6,5},{7,6},{8,7},{9,8},{10,9},{11,1... | collective-permute-start | bytes 589832 | tf_op jit(solution)/shard_map/ppermute | solution.py:19
  28.2 10.3 %collective-permute-start.4 = (bf16[2,128,512]{2,1,0:T(8,128)(2,1)S(1)}, bf16[2,128,512]{2,1,0:T(8,128)(2,1)S(1)}, u32[]{:S(2)}, u32[]{:S(2)}) collective-permute-start(bf16[2,128,512]{2,1,0:T(8,128)(2,1)S(1)} %pad_maximum_fusion.1), channel_id=1, source_target_pairs={{8,0},{9,1},{10,2},{11,3},{12,4},{13,5},{14,6},{15,7},{0,8},{1,9},... | collective-permute-start | bytes 786440 | tf_op jit(solution)/shard_map/ppermute | solution.py:27
  31.4 7.7 %copy-start.2 = (bf16[3,10,96,3,128]{4,1,3,0,2:T(8,128)(2,1)}, bf16[3,10,96,3,128]{4,1,3,0,2:T(8,128)(2,1)S(1)}, u32[]{:S(2)}) copy-start(bf16[3,10,96,3,128]{4,1,3,0,2:T(8,128)(2,1)S(1)} %convert_bitcast_fusion) | copy-start | bytes 6635524
  41.0 1.2 copy-start.6
  42.2 1.7 copy-start.12
  44.0 8.0 %copy-start.7 = (bf16[960,512]{1,0:T(8,128)(2,1)}, bf16[960,512]{1,0:T(8,128)(2,1)S(1)}, u32[]{:S(2)}) copy-start(bf16[960,512]{1,0:T(8,128)(2,1)S(1)} %fusion.19) | copy-start | bytes 2949124
  44.0 4.2 %copy-start.13 = (bf16[1024,512]{1,0:T(8,128)(2,1)S(1)}, bf16[1024,512]{1,0:T(8,128)(2,1)}, u32[]{:S(2)}) copy-start(bf16[1024,512]{1,0:T(8,128)(2,1)} %param.28) | copy-start | bytes 3145732
  44.0 4.2 %copy-start.15 = (bf16[10,96,512]{2,1,0:T(8,128)(2,1)S(1)}, bf16[10,96,512]{2,1,0:T(8,128)(2,1)}, u32[]{:S(2)}) copy-start(bf16[10,96,512]{2,1,0:T(8,128)(2,1)} %param.29) | copy-start | bytes 2949124
  48.1 13.2 %copy-start.16 = (bf16[960,1024]{1,0:T(8,128)(2,1)}, bf16[960,1024]{1,0:T(8,128)(2,1)S(1)}, u32[]{:S(2)}) copy-start(bf16[960,1024]{1,0:T(8,128)(2,1)S(1)} %get-tuple-element.124) | copy-start | bytes 5898244
  51.9 6.1 %copy-start.9 = (bf16[960,512]{1,0:T(8,128)(2,1)}, bf16[960,512]{1,0:T(8,128)(2,1)S(1)}, u32[]{:S(2)}) copy-start(bf16[960,512]{1,0:T(8,128)(2,1)S(1)} %add_convert_fusion) | copy-start | bytes 2949124
  61.4 2.7 copy-start.3
  75.6 10.1 %collective-permute-start.5 = (bf16[2,128,512]{2,1,0:T(8,128)(2,1)S(1)}, bf16[2,128,512]{2,1,0:T(8,128)(2,1)S(1)}, u32[]{:S(2)}, u32[]{:S(2)}) collective-permute-start(bf16[2,128,512]{2,1,0:T(8,128)(2,1)S(1)} %pad_maximum_fusion.2), channel_id=1, source_target_pairs={{8,0},{9,1},{10,2},{11,3},{12,4},{13,5},{14,6},{15,7},{0,8},{1,9},... | collective-permute-start | bytes 786440 | tf_op jit(solution)/shard_map/ppermute | solution.py:27
  86.2 8.6 %collective-permute-start.6 = (bf16[12,16,512]{2,1,0:T(8,128)(2,1)S(1)}, bf16[12,16,512]{2,1,0:T(8,128)(2,1)S(1)}, u32[]{:S(2)}, u32[]{:S(2)}) collective-permute-start(bf16[12,16,512]{2,1,0:T(8,128)(2,1)S(1)} %get-tuple-element.109), channel_id=1, source_target_pairs={{0,1},{1,2},{2,3},{3,4},{4,5},{5,6},{6,7},{7,8},{8,9},{9,10},{10,1... | collective-permute-start | bytes 589832 | tf_op jit(solution)/shard_map/ppermute | solution.py:18
  86.2 8.6 %collective-permute-start.7 = (bf16[12,16,512]{2,1,0:T(8,128)(2,1)S(1)}, bf16[12,16,512]{2,1,0:T(8,128)(2,1)S(1)}, u32[]{:S(2)}, u32[]{:S(2)}) collective-permute-start(bf16[12,16,512]{2,1,0:T(8,128)(2,1)S(1)} %get-tuple-element.110), channel_id=1, source_target_pairs={{1,0},{2,1},{3,2},{4,3},{5,4},{6,5},{7,6},{8,7},{9,8},{10,9},{11,1... | collective-permute-start | bytes 589832 | tf_op jit(solution)/shard_map/ppermute | solution.py:19
  94.9 5.6 %copy-start.17 = (bf16[960,1024]{1,0:T(8,128)(2,1)S(1)}, bf16[960,1024]{1,0:T(8,128)(2,1)}, u32[]{:S(2)}) copy-start(bf16[960,1024]{1,0:T(8,128)(2,1)} %copy-done.16) | copy-start | bytes 5898244
  95.0 5.5 %copy-start.8 = (bf16[960,512]{1,0:T(8,128)(2,1)S(1)}, bf16[960,512]{1,0:T(8,128)(2,1)}, u32[]{:S(2)}) copy-start(bf16[960,512]{1,0:T(8,128)(2,1)} %copy-done.7) | copy-start | bytes 2949124
  95.0 5.5 %copy-start.14 = (bf16[1024,512]{1,0:T(8,128)(2,1)S(1)}, bf16[1024,512]{1,0:T(8,128)(2,1)}, u32[]{:S(2)}) copy-start(bf16[1024,512]{1,0:T(8,128)(2,1)} %param.28) | copy-start | bytes 3145732
  95.2 7.6 %collective-permute-start.8 = (bf16[1,96,512]{2,1,0:T(8,128)(2,1)S(1)}, bf16[1,96,512]{2,1,0:T(8,128)(2,1)S(1)}, u32[]{:S(2)}, u32[]{:S(2)}) collective-permute-start(bf16[1,96,512]{2,1,0:T(8,128)(2,1)S(1)} %get-tuple-element.118), channel_id=1, source_target_pairs={{0,16},{16,32},{32,48},{48,64},{64,80},{80,96},{96,112},{112,128},... | collective-permute-start | bytes 294920 | tf_op jit(solution)/shard_map/ppermute | solution.py:18
  99.2 7.6 %collective-permute-start.9 = (bf16[1,96,512]{2,1,0:T(8,128)(2,1)S(1)}, bf16[1,96,512]{2,1,0:T(8,128)(2,1)S(1)}, u32[]{:S(2)}, u32[]{:S(2)}) collective-permute-start(bf16[1,96,512]{2,1,0:T(8,128)(2,1)S(1)} %get-tuple-element.119), channel_id=1, source_target_pairs={{16,0},{32,16},{48,32},{64,48},{80,64},{96,80},{112,96},{128,112},... | collective-permute-start | bytes 294920 | tf_op jit(solution)/shard_map/ppermute | solution.py:19
  102.6 4.3 %copy-start.10 = (bf16[960,512]{1,0:T(8,128)(2,1)S(1)}, bf16[960,512]{1,0:T(8,128)(2,1)}, u32[]{:S(2)}) copy-start(bf16[960,512]{1,0:T(8,128)(2,1)} %copy-done.9) | copy-start | bytes 2949124
  351.7 3.6 copy-start.5
  355.3 2.0 copy-start.4
  355.3 3.2 copy-start.1
Sparse Core Ops, SparseCore 0:
  72.0 279.6 all-reduce.5
where the time goes:
time: 366 us; the launch traced here: 365 us
  waiting for transfers between devices  275 us (75%)
  matrix products  30.9 us (8%)
  starting transfers between devices  23 us (6%)
  between operations  14.5 us (4%)
  other arithmetic  13 us (4%)
  local copies, waits for them, and re-layouts  8.96 us (2%)
    psum x1, waiting for transfers between devices, local(): lax.psum((mix_local, up_local, down_local), ('lat', 'lon'))  243 us
    ppermute x2, waiting for transfers between devices, shifted(): return lax.ppermute(block, axis, route)  15.9 us
    ppermute x4, waiting for transfers between devices, extended_2(): before = lax.ppermute(last, axis, up)  11.6 us
    ppermute x4, starting transfers between devices, extended_2(): after = lax.ppermute(leading, axis, down)  10.9 us
    ppermute x4, starting transfers between devices, extended_2(): before = lax.ppermute(last, axis, up)  8.71 us
  transfers between devices with their start and end apart: 11, of which 7 were waited for; matrix products, arithmetic and copies ran while one was open for 3% of the time, Pallas kernels for 0%

commit v1 on v0

--- a/solution.py
+++ b/solution.py
@@ -149,7 +149,9 @@
         hidden_grad.astype(jnp.float32).reshape(lat_rows, lon_cols, channels) + adjoint
     ).astype(jnp.bfloat16)
     grad_scale = 1.0 / math.sqrt(points * lat_count * lon_count)
-    mix_total, up_total, down_total = lax.psum((mix_local, up_local, down_local), ("lat", "lon"))
+    mix_total, up_total, down_total = lax.psum(
+        lax.psum((mix_local, up_local, down_local), axis_name="lon"), axis_name="lat"
+    )
     mix_out = (mix_total * grad_scale).astype(jnp.bfloat16)
     up_out = (up_total * grad_scale).astype(jnp.bfloat16)
     down_out = (down_total * grad_scale).astype(jnp.bfloat16)

time: 366 us -> 448 us (1.22)
  waiting for transfers between devices: 275 us -> 366 us
    ppermute x4, waiting for transfers between devices: 11.6 us -> 84.3 us  [extended_2(): before = lax.ppermute(last, axis, up)]
    psum x1 -> x2, waiting for transfers between devices: 243 us -> 264 us  [the longest x1 185 us: local(): lax.psum((mix_local, up_local, down_local), axis_name='lon')]
  transfers between devices with their start and end apart: 11 -> 12, of which waited for: 7 -> 8; matrix products, arithmetic and copies ran while one was open for 3% -> 3% of each run, Pallas kernels for 0% -> 0%
where the time goes in v1:
time: 448 us; the launch traced here: 447 us
  waiting for transfers between devices  366 us (82%)
  matrix products  27.3 us (6%)
  starting transfers between devices  21.8 us (5%)
  between operations  14.5 us (3%)
  other arithmetic  10.5 us (2%)
  local copies, waits for them, and re-layouts  6.95 us (2%)
    psum x1, waiting for transfers between devices, local(): lax.psum((mix_local, up_local, down_local), axis_name='lon')  185 us
    ppermute x4, waiting for transfers between devices, extended_2(): before = lax.ppermute(last, axis, up)  84.3 us
    psum x1, waiting for transfers between devices, local(): lax.psum(lax.psum((mix_local, up_local, down_local), axis_name='lon'), ax...  78.1 us
    ppermute x2, waiting for transfers between devices, shifted(): return lax.ppermute(block, axis, route)  14.7 us
    ppermute x4, starting transfers between devices, extended_2(): after = lax.ppermute(leading, axis, down)  10.9 us
  transfers between devices with their start and end apart: 12, of which 8 were waited for; matrix products, arithmetic and copies ran while one was open for 3% of the time, Pallas kernels for 0%

profile of v1, /device:TPU:8, one launch (start us, length us, event | category | flops | bytes accessed | tf_op | source)
XLA Modules:
  0.0 446.8 jit_solution(6971192744813861346)
XLA Ops:
  7.2 0.0 copy-start
  7.2 0.0 all-reduce.8.cloned.1.call-start
  7.2 1.1 fusion.45
  8.3 1.3 collective-permute-start.1
  9.6 4.6 %collective-permute-start = (bf16[1,96,512]{2,1,0:T(8,128)(2,1)S(1)}, bf16[1,96,512]{2,1,0:T(8,128)(2,1)S(1)}, u32[]{:S(2)}, u32[]{:S(2)}) collective-permute-start(bf16[1,96,512]{2,1,0:T(8,128)(2,1)S(1)} %get-tuple-element.126), channel_id=1, source_target_pairs={{0,16},{16,32},{32,48},{48,64},{64,80},{80,96},{96,112},{112,128},... | collective-permute-start | bytes 294920 | tf_op jit(solution)/shard_map/ppermute | solution.py:18
  14.2 0.7 broadcast_compare_fusion
  14.9 1.4 collective-permute-done
  16.4 1.3 constant_dynamic-update-slice_fusion.1
  17.7 0.1 collective-permute-start.2
  17.8 4.1 collective-permute-start.3
  22.0 6.0 %collective-permute-done.2 = bf16[12,16,512]{2,1,0:T(8,128)(2,1)S(1)} collective-permute-done((bf16[12,16,512]{2,1,0:T(8,128)(2,1)S(1)}, bf16[12,16,512]{2,1,0:T(8,128)(2,1)S(1)}, u32[]{:S(2)}, u32[]{:S(2)}) %collective-permute-start.2) | collective-permute-done | bytes 196640 | tf_op jit(solution)/shard_map/ppermute | solution.py:18
  28.0 0.0 collective-permute-done.3
  28.0 0.2 pad_maximum_fusion
  28.2 2.1 collective-permute-start.4
  30.3 1.1 convert_bitcast_fusion
  31.4 7.1 %collective-permute-done.4 = bf16[2,128,512]{2,1,0:T(8,128)(2,1)S(1)} collective-permute-done((bf16[2,128,512]{2,1,0:T(8,128)(2,1)S(1)}, bf16[2,128,512]{2,1,0:T(8,128)(2,1)S(1)}, u32[]{:S(2)}, u32[]{:S(2)}) %collective-permute-start.4) | collective-permute-done | bytes 262176 | tf_op jit(solution)/shard_map/ppermute | solution.py:27
  38.6 0.4 slice_bitcast_fusion.5
  39.1 1.9 fusion.11
  41.0 0.0 copy-start.6
  41.0 0.2 copy.25
  41.2 1.0 copy-done.6
  42.2 1.7 fusion.19
  44.0 0.0 copy-start.9
  44.0 0.0 copy-start.11
  44.0 4.1 multiply_convert_fusion
  48.1 2.3 fusion.5
  50.4 1.2 add_convert_fusion
  51.6 2.6 fusion.46
  54.3 2.6 fusion.47
  56.9 3.6 fusion.22
  60.5 0.0 all-reduce.8.cloned.1.call-update
  60.5 0.2 all-reduce.10.cloned.1.call-start
  60.7 185.5 %all-reduce.8.cloned.1.call-done = (f32[3,512,512]{2,1,0:T(8,128)}, f32[512,1024]{1,0:T(8,128)}, f32[1024,512]{1,0:T(8,128)}) async-done(((f32[3,512,512]{2,1,0:T(8,128)}, f32[512,1024]{1,0:T(8,128)}, f32[1024,512]{1,0:T(8,128)}), (f32[3,512,512]{2,1,0:T(8,128)}, f32[512,1024]{1,0:T(8,128)}, f32[1024,512]{1,0:T(8,128)})) %all-reduce.8.cloned.1.call-update) | async-done | bytes 7340048 | tf_op jit(solution)/shard_map/psum | solution.py:153
  246.2 0.0 all-reduce.10.cloned.1.call-update
  246.2 1.7 convolution_convert_fusion
  247.9 0.3 copy-done.3
  248.2 2.3 convolution_bitcast_fusion
  250.5 1.5 slice_bitcast_fusion.2
  251.9 1.2 fusion.39
  253.2 2.5 collective-permute-start.5
  255.7 7.5 %collective-permute-done.5 = bf16[2,128,512]{2,1,0:T(8,128)(2,1)S(1)} collective-permute-done((bf16[2,128,512]{2,1,0:T(8,128)(2,1)S(1)}, bf16[2,128,512]{2,1,0:T(8,128)(2,1)S(1)}, u32[]{:S(2)}, u32[]{:S(2)}) %collective-permute-start.5) | collective-permute-done | bytes 262176 | tf_op jit(solution)/shard_map/ppermute | solution.py:27
  263.2 0.1 fusion.31
  263.3 0.1 fusion.29
  263.4 0.2 convert.21
  263.7 0.1 collective-permute-start.6
  263.8 4.1 collective-permute-start.7
  267.9 0.2 slice.334
  268.1 76.9 %collective-permute-done.6 = bf16[12,16,512]{2,1,0:T(8,128)(2,1)S(1)} collective-permute-done((bf16[12,16,512]{2,1,0:T(8,128)(2,1)S(1)}, bf16[12,16,512]{2,1,0:T(8,128)(2,1)S(1)}, u32[]{:S(2)}, u32[]{:S(2)}) %collective-permute-start.6) | collective-permute-done | bytes 196640 | tf_op jit(solution)/shard_map/ppermute | solution.py:18
  345.0 0.0 collective-permute-done.7
  345.0 0.1 fusion.27
  345.1 0.1 fusion.26
  345.2 0.0 copy-start.10
  345.2 0.2 convert.22
  345.4 1.4 collective-permute-start.8
  346.8 1.3 collective-permute-start.9
  348.1 2.1 add_convert_fusion.1
  350.3 0.2 slice.339
  350.4 3.1 collective-permute-done.9
  353.6 1.3 fusion.18
  355.0 78.1 %all-reduce.10.cloned.1.call-done = (f32[3,512,512]{2,1,0:T(8,128)}, f32[512,1024]{1,0:T(8,128)}, f32[1024,512]{1,0:T(8,128)}) async-done(((f32[3,512,512]{2,1,0:T(8,128)}, f32[512,1024]{1,0:T(8,128)}, f32[1024,512]{1,0:T(8,128)}), (f32[3,512,512]{2,1,0:T(8,128)}, f32[512,1024]{1,0:T(8,128)}, f32[1024,512]{1,0:T(8,128)})) %all-reduce.10.cloned.1.call-update) | async-done | bytes 7340048 | tf_op jit(solution)/shard_map/psum | solution.py:152
  433.1 3.6 multiply_convert_fusion.1
  436.7 1.2 multiply_convert_fusion.3
  437.9 0.7 copy-done.4
  438.6 1.3 multiply_convert_fusion.2
  (39 shorter events, 0.5 us)
Async XLA Ops:
  7.2 34.1 %copy-start = (bf16[3,512,512]{2,1,0:T(8,128)(2,1)S(1)}, bf16[3,512,512]{2,1,0:T(8,128)(2,1)}, u32[]{:S(2)}) copy-start(bf16[3,512,512]{2,1,0:T(8,128)(2,1)} %param.26) | copy-start | bytes 4718596
  7.2 14.8 %copy-start.7 = (bf16[3,10,3,33]{3,2,1,0:T(4,128)(2,1)S(1)}, bf16[3,10,3,33]{3,2,1,0:T(4,128)(2,1)}, u32[]{:S(2)}) copy-start(bf16[3,10,3,33]{3,2,1,0:T(4,128)(2,1)} %param.24) | copy-start | bytes 17824
  7.2 239.0 %all-reduce.8.cloned.1.call-start = ((), (), s32[]{:S(2)}) async-start(), calls=%async_computation | async-start | bytes 14680064 | tf_op jit(solution)/shard_map/psum | solution.py:153
  8.3 9.4 %collective-permute-start.1 = (bf16[1,96,512]{2,1,0:T(8,128)(2,1)S(1)}, bf16[1,96,512]{2,1,0:T(8,128)(2,1)S(1)}, u32[]{:S(2)}, u32[]{:S(2)}) collective-permute-start(bf16[1,96,512]{2,1,0:T(8,128)(2,1)S(1)} %get-tuple-element.125), channel_id=1, source_target_pairs={{16,0},{32,16},{48,32},{64,48},{80,64},{96,80},{112,96},{128,112},... | collective-permute-start | bytes 294920 | tf_op jit(solution)/shard_map/ppermute | solution.py:19
  9.6 6.8 %collective-permute-start = (bf16[1,96,512]{2,1,0:T(8,128)(2,1)S(1)}, bf16[1,96,512]{2,1,0:T(8,128)(2,1)S(1)}, u32[]{:S(2)}, u32[]{:S(2)}) collective-permute-start(bf16[1,96,512]{2,1,0:T(8,128)(2,1)S(1)} %get-tuple-element.126), channel_id=1, source_target_pairs={{0,16},{16,32},{32,48},{48,64},{64,80},{80,96},{96,112},{112,128},... | collective-permute-start | bytes 294920 | tf_op jit(solution)/shard_map/ppermute | solution.py:18
  17.7 10.2 %collective-permute-start.2 = (bf16[12,16,512]{2,1,0:T(8,128)(2,1)S(1)}, bf16[12,16,512]{2,1,0:T(8,128)(2,1)S(1)}, u32[]{:S(2)}, u32[]{:S(2)}) collective-permute-start(bf16[12,16,512]{2,1,0:T(8,128)(2,1)S(1)} %get-tuple-element.123), channel_id=1, source_target_pairs={{0,1},{1,2},{2,3},{3,4},{4,5},{5,6},{6,7},{7,8},{8,9},{9,10},{10,1... | collective-permute-start | bytes 589832 | tf_op jit(solution)/shard_map/ppermute | solution.py:18
  17.8 10.2 %collective-permute-start.3 = (bf16[12,16,512]{2,1,0:T(8,128)(2,1)S(1)}, bf16[12,16,512]{2,1,0:T(8,128)(2,1)S(1)}, u32[]{:S(2)}, u32[]{:S(2)}) collective-permute-start(bf16[12,16,512]{2,1,0:T(8,128)(2,1)S(1)} %get-tuple-element.124), channel_id=1, source_target_pairs={{1,0},{2,1},{3,2},{4,3},{5,4},{6,5},{7,6},{8,7},{9,8},{10,9},{11,1... | collective-permute-start | bytes 589832 | tf_op jit(solution)/shard_map/ppermute | solution.py:19
  28.2 10.3 %collective-permute-start.4 = (bf16[2,128,512]{2,1,0:T(8,128)(2,1)S(1)}, bf16[2,128,512]{2,1,0:T(8,128)(2,1)S(1)}, u32[]{:S(2)}, u32[]{:S(2)}) collective-permute-start(bf16[2,128,512]{2,1,0:T(8,128)(2,1)S(1)} %pad_maximum_fusion.1), channel_id=1, source_target_pairs={{8,0},{9,1},{10,2},{11,3},{12,4},{13,5},{14,6},{15,7},{0,8},{1,9},... | collective-permute-start | bytes 786440 | tf_op jit(solution)/shard_map/ppermute | solution.py:27
  31.4 7.7 %copy-start.2 = (bf16[3,10,96,3,128]{4,1,3,0,2:T(8,128)(2,1)}, bf16[3,10,96,3,128]{4,1,3,0,2:T(8,128)(2,1)S(1)}, u32[]{:S(2)}) copy-start(bf16[3,10,96,3,128]{4,1,3,0,2:T(8,128)(2,1)S(1)} %convert_bitcast_fusion) | copy-start | bytes 6635524
  41.0 1.2 copy-start.6
  42.2 1.7 copy-start.8
  44.0 4.2 copy-start.9
  44.0 4.2 copy-start.11
  48.1 6.1 %copy-start.12 = (bf16[960,1024]{1,0:T(8,128)(2,1)}, bf16[960,1024]{1,0:T(8,128)(2,1)S(1)}, u32[]{:S(2)}) copy-start(bf16[960,1024]{1,0:T(8,128)(2,1)S(1)} %get-tuple-element.127) | copy-start | bytes 5898244
  60.5 372.6 %all-reduce.10.cloned.1.call-start = ((), (), s32[]{:S(2)}) async-start(), calls=%async_computation.1 | async-start | bytes 14680064 | tf_op jit(solution)/shard_map/psum | solution.py:152
  246.2 2.0 copy-start.3
  253.2 10.0 %collective-permute-start.5 = (bf16[2,128,512]{2,1,0:T(8,128)(2,1)S(1)}, bf16[2,128,512]{2,1,0:T(8,128)(2,1)S(1)}, u32[]{:S(2)}, u32[]{:S(2)}) collective-permute-start(bf16[2,128,512]{2,1,0:T(8,128)(2,1)S(1)} %pad_maximum_fusion.2), channel_id=1, source_target_pairs={{8,0},{9,1},{10,2},{11,3},{12,4},{13,5},{14,6},{15,7},{0,8},{1,9},... | collective-permute-start | bytes 786440 | tf_op jit(solution)/shard_map/ppermute | solution.py:27
  263.7 81.3 %collective-permute-start.6 = (bf16[12,16,512]{2,1,0:T(8,128)(2,1)S(1)}, bf16[12,16,512]{2,1,0:T(8,128)(2,1)S(1)}, u32[]{:S(2)}, u32[]{:S(2)}) collective-permute-start(bf16[12,16,512]{2,1,0:T(8,128)(2,1)S(1)} %get-tuple-element.112), channel_id=1, source_target_pairs={{0,1},{1,2},{2,3},{3,4},{4,5},{5,6},{6,7},{7,8},{8,9},{9,10},{10,1... | collective-permute-start | bytes 589832 | tf_op jit(solution)/shard_map/ppermute | solution.py:18
  263.8 81.3 %collective-permute-start.7 = (bf16[12,16,512]{2,1,0:T(8,128)(2,1)S(1)}, bf16[12,16,512]{2,1,0:T(8,128)(2,1)S(1)}, u32[]{:S(2)}, u32[]{:S(2)}) collective-permute-start(bf16[12,16,512]{2,1,0:T(8,128)(2,1)S(1)} %get-tuple-element.113), channel_id=1, source_target_pairs={{1,0},{2,1},{3,2},{4,3},{5,4},{6,5},{7,6},{8,7},{9,8},{10,9},{11,1... | collective-permute-start | bytes 589832 | tf_op jit(solution)/shard_map/ppermute | solution.py:19
  345.2 2.9 copy-start.10
  345.2 2.9 copy-start.13
  345.4 5.0 %collective-permute-start.8 = (bf16[1,96,512]{2,1,0:T(8,128)(2,1)S(1)}, bf16[1,96,512]{2,1,0:T(8,128)(2,1)S(1)}, u32[]{:S(2)}, u32[]{:S(2)}) collective-permute-start(bf16[1,96,512]{2,1,0:T(8,128)(2,1)S(1)} %get-tuple-element.121), channel_id=1, source_target_pairs={{0,16},{16,32},{32,48},{48,64},{64,80},{80,96},{96,112},{112,128},... | collective-permute-start | bytes 294920 | tf_op jit(solution)/shard_map/ppermute | solution.py:18
  346.8 6.7 %collective-permute-start.9 = (bf16[1,96,512]{2,1,0:T(8,128)(2,1)S(1)}, bf16[1,96,512]{2,1,0:T(8,128)(2,1)S(1)}, u32[]{:S(2)}, u32[]{:S(2)}) collective-permute-start(bf16[1,96,512]{2,1,0:T(8,128)(2,1)S(1)} %get-tuple-element.122), channel_id=1, source_target_pairs={{16,0},{32,16},{48,32},{64,48},{80,64},{96,80},{112,96},{128,112},... | collective-permute-start | bytes 294920 | tf_op jit(solution)/shard_map/ppermute | solution.py:19
  433.1 3.6 copy-start.5
  436.7 2.0 copy-start.4
  436.7 3.2 copy-start.1
Sparse Core Ops, SparseCore 0:
  60.6 185.5 all-reduce.7
  249.0 183.9 all-reduce.9
